TPU v7x, 32 devices: a whole 2x2x4 slice. The times are simulated.
32 devices in a mesh: groups: 2 (over y), blk: 4 (over z), leaf: 2 (over x), sample: 2 (over core).
Axes of the slice: x: 2, y: 2, z: 4, core: 2. Of those that a mesh axis runs over, the one named last changes fastest.
Arguments:
- residual: float32 [256, 128, 256], P(('groups', 'blk', 'leaf'), 'sample'), parts along dimension 0, may hold values from -60 to 60
- direction: bfloat16 [256, 128, 256], P(('groups', 'blk', 'leaf'), 'sample'), parts along dimension 0, may hold values from -60 to 60
- step: float32 [256], P(('groups', 'sample')), parts along dimension 0, may hold values from 0.2 to 0.8
- coords: bfloat16 [256, 3, 256], P(('groups', 'blk', 'leaf')), parts along dimension 0, may hold values from 0 to 1
- order: int32 [256, 256], P(('groups', 'blk', 'leaf')), parts along dimension 0, may hold values from 0 to 255, each once within a row
- basis: bfloat16 [256, 64, 256], P(('groups', 'blk', 'leaf')), parts along dimension 0, may hold values from -0.5 to 0.5
- leaf_transfer: bfloat16 [256, 64, 64], P(('groups', 'blk', 'leaf')), parts along dimension 0, may hold values from -0.75 to 0.75
- node_transfer: bfloat16 [16, 64, 64], P(('groups', 'blk', 'leaf')), parts along dimension 0, may hold values from -0.75 to 0.75
- near_list: int32 [256, 12], P(('groups', 'blk', 'leaf')), parts along dimension 0, may hold values from 0 to 127, as said below
- coupling_list: int32 [256, 8], P(('groups', 'blk', 'leaf')), parts along dimension 0, may hold values from 0 to 127, as said below
- coupling: bfloat16 [256, 8, 64, 64], P(('groups', 'blk', 'leaf')), parts along dimension 0, may hold values from -0.25 to 0.25
- top_list: int32 [8, 4], P(('groups', 'blk')), parts along dimension 0, may hold values from 0 to 3, as said below
- top_coupling: bfloat16 [8, 4, 64, 64], P(('groups', 'blk')), parts along dimension 0, may hold values from -0.0625 to 0.0625
Outputs:
- residual_next: float32 [256, 128, 256], P(('groups', 'blk', 'leaf'), 'sample'), parts along dimension 0
- direction_next: bfloat16 [256, 128, 256], P(('groups', 'blk', 'leaf'), 'sample'), parts along dimension 0
There are 2 independent parts, one for each index of `groups`. A program takes and returns all parts, laid end to end along the dimension named above; each array names one. Nothing has to cross between parts.
Inputs may be any that keep to these rules, and one draw needn't show every extreme that they name: `near_list`: entry 0 of leaf g is g itself; the other entries are distinct leaves other than g, each at most 16 positions from g around the cycle of 128 leaves; some leaf names both g - 16 and g + 16 (mod 128). `coupling_list`: the entries of leaf g are distinct leaves of the aligned blocks of 16 leaves just before and just after g's own block, around the cycle of 128 leaves, each more than 16 positions from g. `top_list`: the entries of top cluster b name clusters other than b; they may repeat.
All inputs are finite; a program needn't handle non-finite values.
Results may differ from a plain program's by a relative error of at most 0.0065.
Values may be sent and summed in bfloat16 or wider, within the bound.
No kernel may reach another device: no remote copies, remote signals or barrier semaphores. Data moves between devices by JAX's collectives and lax.ppermute only.
A program may use at most 64 MiB of HBM per device.

v0:
```python
import math
import jax
import jax.numpy as jnp
from jax import lax
from jax.sharding import PartitionSpec as P

LEAF_DEV = 16
ROOT_THREE = math.sqrt(3.0)
LENGTH = 0.3
AMPLITUDE = 0.25
NUGGET = 0.5


def padded(array, sides, width):
    for axis, dim in sides:
        count, length = (lax.axis_size(axis), array.shape[dim])
        up = [(i, (i + 1) % count) for i in range(count)]
        down = [(j, i) for i, j in up]
        last = lax.slice_in_dim(array, length - width, length, axis=dim)
        initial = lax.slice_in_dim(array, 0, width, axis=dim)
        before = lax.ppermute(last, axis, up)
        after = lax.ppermute(initial, axis, down)
        array = jnp.concatenate([before, array, after], axis=dim)
    return array


def swapped(array, axis, bit):
    return lax.ppermute(array, axis, [(i, i ^ 1 << bit) for i in range(lax.axis_size(axis))])


def matern(own_offsets, near_offsets, gap_leaves, spread):
    gap_x = (
        own_offsets[0][:, None] - near_offsets[0][None, :] + gap_leaves.astype(jnp.float32) * spread
    )
    gap_y = own_offsets[1][:, None] - near_offsets[1][None, :]
    gap_z = own_offsets[2][:, None] - near_offsets[2][None, :]
    scaled = jnp.sqrt(gap_x * gap_x + gap_y * gap_y + gap_z * gap_z) * (ROOT_THREE / LENGTH)
    return AMPLITUDE * (1.0 + scaled) * jnp.exp(-scaled)


def tile_block(own_offsets, near_offsets, gap_leaves, spread):
    inner = jax.vmap(matern, in_axes=(None, 0, 0, None))
    return jax.vmap(inner, in_axes=(0, 0, 0, None))(own_offsets, near_offsets, gap_leaves, spread)


def on_device(
    residual,
    direction,
    step,
    coords,
    order,
    basis,
    leaf_transfer,
    node_transfer,
    near_list,
    coupling_list,
    coupling,
    top_list,
    top_coupling,
):
    leaf_dev = direction.shape[0]
    samples = direction.shape[1]
    points = direction.shape[2]
    blk_count = lax.axis_size("blk")
    leaf_count = lax.axis_size("leaf")
    leaf_total = leaf_dev * blk_count * leaf_count
    device = lax.axis_index("blk") * leaf_count + lax.axis_index("leaf")
    first_leaf = device * leaf_dev
    spread = 0.5 / LEAF_DEV
    old_norm = lax.psum(jnp.sum(residual * residual, axis=(0, 2)), ("blk", "leaf"))
    packed = jnp.concatenate([direction, coords], axis=1)
    widened = padded(packed, ((("blk", "leaf"), 0),), leaf_dev)
    anchor = first_leaf - leaf_dev
    own_offsets_all = coords.astype(jnp.float32)
    slot_ids = jnp.mod(near_list - anchor, leaf_total)
    window_values = widened[:, :samples, :]
    window_offsets = widened[:, samples:, :]
    half_rows = leaf_dev // 2
    side = lax.axis_index("sample")
    partner_values = swapped(window_values, "sample", 0)
    all_columns = jnp.where(
        side == 0,
        jnp.concatenate([window_values, partner_values], axis=1),
        jnp.concatenate([partner_values, window_values], axis=1),
    )
    base = side * half_rows
    blocks = 4
    columns = all_columns.shape[1]

    def near_block(block_index):
        start_at = base + block_index * blocks
        slot_rows = lax.dynamic_slice_in_dim(slot_ids, start_at, blocks, 0)
        name_rows = lax.dynamic_slice_in_dim(near_list, start_at, blocks, 0)
        leaf_ids = first_leaf + start_at + jnp.arange(blocks, dtype=jnp.int32)
        near_values = all_columns[slot_rows]
        near_offsets = window_offsets[slot_rows].astype(jnp.float32)
        own_offsets = lax.dynamic_slice_in_dim(own_offsets_all, start_at, blocks, 0)
        gap_leaves = (
            jnp.mod(leaf_ids[:, None] - name_rows + leaf_total // 2, leaf_total) - leaf_total // 2
        )
        kernel_tiles = tile_block(own_offsets, near_offsets, gap_leaves, spread).astype(
            jnp.bfloat16
        )
        return jnp.einsum(
            "lkab,lksb->lsa", kernel_tiles, near_values, preferred_element_type=jnp.float32
        )

    mapped = lax.map(near_block, jnp.arange(half_rows // blocks, dtype=jnp.int32))
    own_rows = mapped.reshape(half_rows, columns, points)
    kept_part = lax.dynamic_slice_in_dim(own_rows, side * samples, samples, 1)
    given_part = lax.dynamic_slice_in_dim(own_rows, (1 - side) * samples, samples, 1)
    received = swapped(given_part.astype(jnp.bfloat16), "sample", 0).astype(given_part.dtype)
    near_field = jnp.where(
        side == 0,
        jnp.concatenate([kept_part, received], axis=0),
        jnp.concatenate([received, kept_part], axis=0),
    )
    inverse = jnp.argsort(order, axis=1)
    natural_values = jnp.take_along_axis(basis, inverse[:, None, :], axis=2)
    expansion_weights = jnp.einsum(
        "ejt,ekt->ekj", natural_values, direction, preferred_element_type=jnp.float32
    ).astype(jnp.bfloat16)
    node_coef = jnp.einsum(
        "lrk,lsk->sr", leaf_transfer, expansion_weights, preferred_element_type=jnp.float32
    ).astype(jnp.bfloat16)
    lifted = jnp.einsum(
        "rk,sk->sr", node_transfer[0], node_coef, preferred_element_type=jnp.float32
    )
    top_node = lax.psum(lifted, "leaf").astype(jnp.bfloat16)
    every_top = lax.all_gather(top_node[None], "blk", axis=0, tiled=True)
    chosen = every_top[top_list[0]]
    incoming = jnp.einsum(
        "krj,ksj->sr", top_coupling[0], chosen, preferred_element_type=jnp.float32
    )
    incoming = incoming.astype(jnp.bfloat16)
    down_coef = jnp.einsum(
        "rk,sr->sk", node_transfer[0], incoming, preferred_element_type=jnp.float32
    ).astype(jnp.bfloat16)
    coef_wide = padded(expansion_weights, ((("blk", "leaf"), 0),), leaf_dev)
    paired_block = coef_wide[jnp.mod(coupling_list - (first_leaf - leaf_dev), leaf_total)]
    upward_gathered = jnp.einsum(
        "lrk,sr->lsk", leaf_transfer, down_coef, preferred_element_type=jnp.float32
    )
    upward_gathered = upward_gathered + jnp.einsum(
        "ohvd,ohgd->ogv", coupling, paired_block, preferred_element_type=jnp.float32
    )
    upward_gathered = upward_gathered.astype(jnp.bfloat16)
    distant_field = jnp.einsum(
        "bfw,baf->baw", natural_values, upward_gathered, preferred_element_type=jnp.float32
    )
    product_image = NUGGET * direction.astype(jnp.float32) + near_field + distant_field
    residual_next = residual - step[None, :, None] * product_image
    new_square = jnp.sum(residual_next * residual_next, axis=(0, 2))
    new_norm = lax.psum(new_square, ("blk", "leaf"))
    beta_ratio = new_norm / old_norm
    direction_next = (
        residual_next + beta_ratio[None, :, None] * direction.astype(jnp.float32)
    ).astype(jnp.bfloat16)
    return (residual_next, direction_next)


def solution(mesh):
    in_specs = (
        P(("groups", "blk", "leaf"), "sample", None),
        P(("groups", "blk", "leaf"), "sample", None),
        P(("groups", "sample")),
        P(("groups", "blk", "leaf"), None, None),
        P(("groups", "blk", "leaf"), None),
        P(("groups", "blk", "leaf"), None, None),
        P(("groups", "blk", "leaf"), None, None),
        P(("groups", "blk", "leaf"), None, None),
        P(("groups", "blk", "leaf"), None),
        P(("groups", "blk", "leaf"), None),
        P(("groups", "blk", "leaf"), None, None, None),
        P(("groups", "blk"), None),
        P(("groups", "blk"), None, None, None),
    )
    out_specs = (
        P(("groups", "blk", "leaf"), "sample", None),
        P(("groups", "blk", "leaf"), "sample", None),
    )
    return jax.shard_map(
        on_device, mesh=mesh, in_specs=in_specs, out_specs=out_specs, check_vma=False
    )
```

profile of v0, /device:TPU:0, one launch (start us, length us, event | category | flops | bytes accessed | tf_op | source)
XLA Modules:
  0.0 217.3 jit_solution(16189384715876912534)
XLA Ops:
  7.2 1.5 copy_dynamic-update-slice_fusion
  8.7 1.4 fusion.37
  10.1 2.9 %collective-permute-start = (bf16[16,67,256]{2,0,1:T(8,128)(2,1)S(1)}, bf16[16,67,256]{2,0,1:T(8,128)(2,1)S(1)}, u32[]{:S(2)}, u32[]{:S(2)}) collective-permute-start(bf16[16,67,256]{2,0,1:T(8,128)(2,1)S(1)} %get-tuple-element.173), channel_id=1, source_target_pairs={{0,2},{2,4},{4,6},{6,8},{8,10},{10,12},{12,14},{14,0},{1,3},{3,5},... | collective-permute-start | bytes 1646600 | tf_op jit(solution)/shard_map/ppermute | solution.py:21
  13.1 3.0 %collective-permute-start.1 = (bf16[16,67,256]{2,0,1:T(8,128)(2,1)S(1)}, bf16[16,67,256]{2,0,1:T(8,128)(2,1)}, u32[]{:S(2)}, u32[]{:S(2)}) collective-permute-start(bf16[16,67,256]{2,0,1:T(8,128)(2,1)S(1)} %get-tuple-element.173), channel_id=1, source_target_pairs={{2,0},{4,2},{6,4},{8,6},{10,8},{12,10},{14,12},{0,14},{3,1},{5,3},... | collective-permute-start | bytes 1646600 | tf_op jit(solution)/shard_map/ppermute | solution.py:22
  17.6 1.9 multiply_reduce_fusion
  20.2 16.4 %collective-permute-done = bf16[16,67,256]{2,0,1:T(8,128)(2,1)S(1)} collective-permute-done((bf16[16,67,256]{2,0,1:T(8,128)(2,1)S(1)}, bf16[16,67,256]{2,0,1:T(8,128)(2,1)S(1)}, u32[]{:S(2)}, u32[]{:S(2)}) %collective-permute-start) | collective-permute-done | bytes 548896 | tf_op jit(solution)/shard_map/ppermute | solution.py:21
  36.5 2.3 %collective-permute-done.1 = bf16[16,67,256]{2,0,1:T(8,128)(2,1)} collective-permute-done((bf16[16,67,256]{2,0,1:T(8,128)(2,1)S(1)}, bf16[16,67,256]{2,0,1:T(8,128)(2,1)}, u32[]{:S(2)}, u32[]{:S(2)}) %collective-permute-start.1) | collective-permute-done | bytes 548896 | tf_op jit(solution)/shard_map/ppermute | solution.py:22
  38.9 1.2 pad_maximum_fusion
  40.0 1.3 slice.57
  43.1 1.5 copy.38
  45.4 40.6 %gather_fusion.4 = bf16[4096,64]{1,0:T(8,128)(2,1)} fusion(bf16[16,64,256]{1,2,0:T(8,128)(2,1)S(1)} %copy.38, s32[4096]{0:T(1024)S(1)} %bitcast.104), kind=kCustom, calls=%fused_computation.4 | custom fusion | bytes 1081344 | tf_op jit(solution)/shard_map/jit(take_along_axis)/gather | solution.py:119
  86.0 2.4 %copy.39 = bf16[16,256,64]{1,2,0:T(8,128)(2,1)} copy(bf16[16,256,64]{2,1,0:T(8,128)(2,1)} %bitcast.109) | data formatting | bytes 1048576 | tf_op jit(solution)/shard_map/jit(take_along_axis)/gather | solution.py:119
  88.4 2.2 %fusion.12 = bf16[16,64,64]{1,2,0:T(8,128)(2,1)} fusion(bf16[16,64,256]{2,1,0:T(8,128)(2,1)} %param.16, bf16[16,256,64]{1,2,0:T(8,128)(2,1)} %copy.39, pred[16,256]{1,0:T(8,128)(4,1)S(1)} %compare_and_fusion), kind=kOutput, calls=%fused_computation.37 | convolution fusion | flops 33882112 | bytes 1183744 | tf_op jit(solution)/shard_map/ejt,ekt->ekj/dot_general | solution.py:120
  91.0 4.3 %collective-permute-start.5 = (bf16[16,64,64]{1,2,0:T(8,128)(2,1)}, bf16[16,64,64]{1,2,0:T(8,128)(2,1)}, u32[]{:S(2)}, u32[]{:S(2)}) collective-permute-start(bf16[16,64,64]{1,2,0:T(8,128)(2,1)} %fusion.12), channel_id=1, source_target_pairs={{2,0},{4,2},{6,4},{8,6},{10,8},{12,10},{14,12},{0,14},{3,1},{5,3},... | collective-permute-start | bytes 393224 | tf_op jit(solution)/shard_map/ppermute | solution.py:22
  95.4 1.3 fusion.17
  96.7 11.0 %psum.21 = bf16[64,64]{1,0:T(8,128)(2,1)S(1)} all-reduce(f32[64,64]{1,0:T(8,128)S(1)} %fusion.17), channel_id=1, replica_groups=mesh['groups'=2,'blk'=4,'leaf'=2,'sample'=2] {'leaf'}, use_global_device_ids=true, to_apply=%region_3.4 | all-reduce | flops 4096 | bytes 24576 | tf_op jit(solution)/shard_map/psum | solution.py:129
  107.7 13.5 %all-gather = bf16[256,64]{1,0:T(8,128)(2,1)S(1)} all-gather(bf16[64,64]{1,0:T(8,128)(2,1)S(1)} %psum.21), channel_id=2, replica_groups=mesh['groups'=2,'blk'=4,'leaf'=2,'sample'=2] {'blk'}, dimensions={0}, use_global_device_ids=true | all-gather | bytes 40960 | tf_op jit(solution)/shard_map/all_gather | solution.py:130
  121.2 1.3 gather_fusion.2
  124.5 3.1 %maximum_select_fusion = bf16[48,128,256]{2,0,1:T(8,128)(2,1)S(1)} fusion(bf16[48,64,256]{2,0,1:T(8,128)(2,1)} %collective-permute-done.2, bf16[48,64,256]{2,0,1:T(8,128)(2,1)} %slice.57, pred[]{:T(512)S(6)} %eq.12), kind=kLoop, calls=%fused_computation.28 | loop fusion | flops 4718592 | bytes 6291457 | tf_op jit(solution)/shard_map/jit(_where)/select_n | solution.py:81
  127.7 2.8 %copy.36 = bf16[48,128,256]{2,1,0:T(8,128)(2,1)} copy(bf16[48,128,256]{2,0,1:T(8,128)(2,1)S(1)} %maximum_select_fusion) | data formatting | bytes 6291456 | tf_op jit(solution)/shard_map/while | solution.py:108
  130.4 42.3 %while.12 = (s32[]{:T(128)}, f32[2,4,128,256]{3,2,1,0:T(8,128)}, s32[2]{0:T(128)S(1)}, s32[]{:T(128)}, s32[16,12]{1,0:T(8,128)}, /*index=5*/bf16[48,128,256]{2,1...) while((s32[]{:T(128)}, f32[2,4,128,256]{3,2,1,0:T(8,128)}, ...), condition=%wide.region_1.0_spmd, body=%wide.region_0.0_spmd.sunk | while | flops 852494208 | bytes 11184823 | solution.py:108
  134.2 4.4 %gather_fusion = bf16[48,128,256]{2,1,0:T(8,128)(2,1)} fusion(bf16[48,128,256]{2,1,0:T(8,128)(2,1)} %get-tuple-element.290, s32[1024]{0:T(1024)S(1)} %pad_clamp_fusion.4), kind=kCustom, calls=%fused_computation.clone.1 | custom fusion | bytes 6291648 | tf_op jit(solution)/shard_map/while/body/eval_jaxpr/gather | solution.py:95
  139.4 12.2 %fusion.54 = f32[2,4,128,256]{3,2,1,0:T(8,128)} fusion(f32[2,4,128,256]{3,2,1,0:T(8,128)} %get-tuple-element.270, s32[]{:T(128)} %get-tuple-element.269, bf16[4,12,128,256]{3,2,1,0:T(8,128)(2,1)} %bitcast.105, f32[4,12,256]{2,1,0:T(8,128)S(1)} %copy.62, f32[4,256]{1,0:T(4,128)S(1)} %get-tuple-element.248, f32[4,12,256]{2,1,0:T(8,128)S(1)} %copy.63, ...), kind=kOutput, calls=%fused_computation.8.clone.1 | convolution fusion | flops 852492288 | bytes 3830464 | tf_op jit(solution)/shard_map/while/body/eval_jaxpr/lkab,lksb->lsa/dot_general | solution.py:104
  155.4 4.4 %gather_fusion = bf16[48,128,256]{2,1,0:T(8,128)(2,1)} fusion(bf16[48,128,256]{2,1,0:T(8,128)(2,1)} %get-tuple-element.290, s32[1024]{0:T(1024)S(1)} %pad_clamp_fusion.4), kind=kCustom, calls=%fused_computation.clone.1 | custom fusion | bytes 6291648 | tf_op jit(solution)/shard_map/while/body/eval_jaxpr/gather | solution.py:95
  160.6 12.1 %fusion.54 = f32[2,4,128,256]{3,2,1,0:T(8,128)} fusion(f32[2,4,128,256]{3,2,1,0:T(8,128)} %get-tuple-element.270, s32[]{:T(128)} %get-tuple-element.269, bf16[4,12,128,256]{3,2,1,0:T(8,128)(2,1)} %bitcast.105, f32[4,12,256]{2,1,0:T(8,128)S(1)} %copy.62, f32[4,256]{1,0:T(4,128)S(1)} %get-tuple-element.248, f32[4,12,256]{2,1,0:T(8,128)S(1)} %copy.63, ...), kind=kOutput, calls=%fused_computation.8.clone.1 | convolution fusion | flops 852492288 | bytes 3830464 | tf_op jit(solution)/shard_map/while/body/eval_jaxpr/lkab,lksb->lsa/dot_general | solution.py:104
  172.7 1.8 dynamic-slice_convert_fusion
  175.5 1.3 pad_maximum_fusion.1
  176.8 2.1 gather_fusion.3
  179.0 1.9 constant_dynamic-slice_fusion
  181.9 4.6 %multiply_reduce_fusion.1 = (f32[64]{0:T(128)S(1)}, f32[16,64,256]{2,1,0:T(8,128)}) fusion(f32[16,64,256]{2,1,0:T(8,128)} %param.15, bf16[16,256,64]{1,2,0:T(8,128)(2,1)} %copy.39, pred[16,256]{1,0:T(8,128)(4,1)S(1)} %copy-done.12, f32[16,64,64]{2,1,0:T(8,128)} %convolution_bitcast_fusion.1, bf16[16,8,64,64]{2,3,1,0:T(8,128)(2,1)} %bitcast.107, ...), kind=kOutput, calls=%fused_computation.54 | convolution fusion | flops 103940032 | bytes 6558209 | tf_op jit(solution)/shard_map/bfw,baf->baw/dot_general | solution.py:148
  186.5 21.7 %all-reduce = (f32[64]{0:T(128)S(1)}, f32[64]{0:T(128)S(1)}) all-reduce(f32[64]{0:T(128)S(1)} %get-tuple-element.174, f32[64]{0:T(128)S(1)} %copy-done.14), channel_id=1, replica_groups=mesh['groups'=2,'blk'=4,'leaf'=2,'sample'=2] {'blk','leaf'}, use_global_device_ids=true, to_apply=%region_5.6 | all-reduce | flops 128 | bytes 1024 | tf_op jit(solution)/shard_map/psum | solution.py:154
  208.2 2.2 %fusion.23 = bf16[16,64,256]{2,1,0:T(8,128)(2,1)} fusion(f32[16,64,256]{2,1,0:T(8,128)} %get-tuple-element.175, bf16[16,64,256]{2,1,0:T(8,128)(2,1)S(1)} %copy-done.3, f32[64]{0:T(128)S(1)} %div.3), kind=kLoop, calls=%fused_computation.51 | loop fusion | flops 1048576 | bytes 2097408 | tf_op jit(solution)/shard_map/convert_element_type | solution.py:158
  (87 shorter events, 16.8 us)
Async XLA Ops:
  7.2 174.7 %copy-start = (bf16[16,8,64,64]{3,2,1,0:T(8,128)(2,1)S(1)}, bf16[16,8,64,64]{3,2,1,0:T(8,128)(2,1)}, u32[]{:S(2)}) copy-start(bf16[16,8,64,64]{3,2,1,0:T(8,128)(2,1)} %param.25) | copy-start | bytes 3145732
  7.2 37.5 %sort.19.cloned.1.call-start = ((), (), s32[]{:S(2)}) async-start(), calls=%async_computation | async-start | bytes 98336 | tf_op jit(solution)/shard_map/jit(argsort)/sort | solution.py:118
  10.1 31.2 %copy-start.1 = (bf16[16,67,256]{2,0,1:T(8,128)(2,1)}, bf16[16,67,256]{2,0,1:T(8,128)(2,1)S(1)}, u32[]{:S(2)}) copy-start(bf16[16,67,256]{2,0,1:T(8,128)(2,1)S(1)} %get-tuple-element.173) | copy-start | bytes 1646596
  10.1 26.4 %collective-permute-start = (bf16[16,67,256]{2,0,1:T(8,128)(2,1)S(1)}, bf16[16,67,256]{2,0,1:T(8,128)(2,1)S(1)}, u32[]{:S(2)}, u32[]{:S(2)}) collective-permute-start(bf16[16,67,256]{2,0,1:T(8,128)(2,1)S(1)} %get-tuple-element.173), channel_id=1, source_target_pairs={{0,2},{2,4},{4,6},{6,8},{8,10},{10,12},{12,14},{14,0},{1,3},{3,5},... | collective-permute-start | bytes 1646600 | tf_op jit(solution)/shard_map/ppermute | solution.py:21
  13.1 25.8 %collective-permute-start.1 = (bf16[16,67,256]{2,0,1:T(8,128)(2,1)S(1)}, bf16[16,67,256]{2,0,1:T(8,128)(2,1)}, u32[]{:S(2)}, u32[]{:S(2)}) collective-permute-start(bf16[16,67,256]{2,0,1:T(8,128)(2,1)S(1)} %get-tuple-element.173), channel_id=1, source_target_pairs={{2,0},{4,2},{6,4},{8,6},{10,8},{12,10},{14,12},{0,14},{3,1},{5,3},... | collective-permute-start | bytes 1646600 | tf_op jit(solution)/shard_map/ppermute | solution.py:22
  20.2 21.7 %copy-start.9 = (s32[16,12]{1,0:T(8,128)S(1)}, s32[16,12]{1,0:T(8,128)}, u32[]{:S(2)}) copy-start(s32[16,12]{1,0:T(8,128)} %param.23) | copy-start | bytes 2308
  36.5 4.8 %copy-start.4 = (bf16[16,67,256]{2,0,1:T(8,128)(2,1)}, bf16[16,67,256]{2,0,1:T(8,128)(2,1)S(1)}, u32[]{:S(2)}) copy-start(bf16[16,67,256]{2,0,1:T(8,128)(2,1)S(1)} %collective-permute-done) | copy-start | bytes 1646596
  41.3 83.2 %collective-permute-start.2 = (bf16[48,64,256]{2,0,1:T(8,128)(2,1)}, bf16[48,64,256]{2,0,1:T(8,128)(2,1)}, u32[]{:S(2)}, u32[]{:S(2)}) collective-permute-start(bf16[48,64,256]{2,0,1:T(8,128)(2,1)} %slice.57), channel_id=1, source_target_pairs={{0,1},{1,0},{2,3},{3,2},{4,5},{5,4},{6,7},{7,6},{8,9},{9,8},{10,11... | collective-permute-start | bytes 4718600 | tf_op jit(solution)/shard_map/ppermute | solution.py:28
  45.4 43.0 %copy-start.8 = (s32[16,256]{1,0:T(8,128)S(1)}, s32[16,256]{1,0:T(8,128)}, u32[]{:S(2)}) copy-start(s32[16,256]{1,0:T(8,128)} %get-tuple-element.131) | copy-start | bytes 49156
  45.4 50.0 %copy-start.7 = (bf16[1,64,64]{2,1,0:T(8,128)(2,1)S(1)}, bf16[1,64,64]{2,1,0:T(8,128)(2,1)}, u32[]{:S(2)}) copy-start(bf16[1,64,64]{2,1,0:T(8,128)(2,1)} %param.22) | copy-start | bytes 24580
  86.0 9.4 %copy-start.6 = (bf16[16,64,64]{2,1,0:T(8,128)(2,1)S(1)}, bf16[16,64,64]{2,1,0:T(8,128)(2,1)}, u32[]{:S(2)}) copy-start(bf16[16,64,64]{2,1,0:T(8,128)(2,1)} %param.21) | copy-start | bytes 393220
  86.0 37.7 %copy-start.2 = (bf16[16,67,256]{2,0,1:T(8,128)(2,1)S(1)}, bf16[16,67,256]{2,0,1:T(8,128)(2,1)}, u32[]{:S(2)}) copy-start(bf16[16,67,256]{2,0,1:T(8,128)(2,1)} %copy-done.1) | copy-start | bytes 1646596
  86.0 37.7 %copy-start.5 = (bf16[16,67,256]{2,0,1:T(8,128)(2,1)S(1)}, bf16[16,67,256]{2,0,1:T(8,128)(2,1)}, u32[]{:S(2)}) copy-start(bf16[16,67,256]{2,0,1:T(8,128)(2,1)} %copy-done.4) | copy-start | bytes 1646596
  88.4 2.6 %copy-start.11 = (pred[16,256]{1,0:T(8,128)(4,1)}, pred[16,256]{1,0:T(8,128)(4,1)S(1)}, u32[]{:S(2)}) copy-start(pred[16,256]{1,0:T(8,128)(4,1)S(1)} %compare_and_fusion) | copy-start | bytes 12292
  90.6 84.9 %collective-permute-start.4 = (bf16[16,64,64]{1,2,0:T(8,128)(2,1)}, bf16[16,64,64]{1,2,0:T(8,128)(2,1)}, u32[]{:S(2)}, u32[]{:S(2)}) collective-permute-start(bf16[16,64,64]{1,2,0:T(8,128)(2,1)} %fusion.12), channel_id=1, source_target_pairs={{0,2},{2,4},{4,6},{6,8},{8,10},{10,12},{12,14},{14,0},{1,3},{3,5},... | collective-permute-start | bytes 393224 | tf_op jit(solution)/shard_map/ppermute | solution.py:21
  91.0 84.5 %collective-permute-start.5 = (bf16[16,64,64]{1,2,0:T(8,128)(2,1)}, bf16[16,64,64]{1,2,0:T(8,128)(2,1)}, u32[]{:S(2)}, u32[]{:S(2)}) collective-permute-start(bf16[16,64,64]{1,2,0:T(8,128)(2,1)} %fusion.12), channel_id=1, source_target_pairs={{2,0},{4,2},{6,4},{8,6},{10,8},{12,10},{14,12},{0,14},{3,1},{5,3},... | collective-permute-start | bytes 393224 | tf_op jit(solution)/shard_map/ppermute | solution.py:22
  130.4 46.4 %copy-start.10 = (s32[1024]{0:T(1024)S(1)}, s32[1024]{0:T(1024)}, u32[]{:S(2)}) copy-start(s32[1024]{0:T(1024)} %pad_clamp_fusion.1) | copy-start | bytes 12292
  174.5 6.4 %collective-permute-start.3 = (bf16[8,64,256]{2,1,0:T(8,128)(2,1)}, bf16[8,64,256]{2,1,0:T(8,128)(2,1)}, u32[]{:S(2)}, u32[]{:S(2)}) collective-permute-start(bf16[8,64,256]{2,1,0:T(8,128)(2,1)} %dynamic-slice_convert_fusion), channel_id=1, source_target_pairs={{0,1},{1,0},{2,3},{3,2},{4,5},{5,4},{6,7},{7,6},{8,9},{9,8},{10,11... | collective-permute-start | bytes 786440 | tf_op jit(solution)/shard_map/ppermute | solution.py:28
  176.8 5.1 %copy-start.3 = (bf16[16,64,256]{2,1,0:T(8,128)(2,1)S(1)}, bf16[16,64,256]{2,1,0:T(8,128)(2,1)}, u32[]{:S(2)}) copy-start(bf16[16,64,256]{2,1,0:T(8,128)(2,1)} %param.16) | copy-start | bytes 1572868
  176.8 5.1 %copy-start.12 = (pred[16,256]{1,0:T(8,128)(4,1)S(1)}, pred[16,256]{1,0:T(8,128)(4,1)}, u32[]{:S(2)}) copy-start(pred[16,256]{1,0:T(8,128)(4,1)} %copy-done.11) | copy-start | bytes 12292
  176.8 5.1 %copy-start.13 = (f32[64]{0:T(128)S(1)}, f32[64]{0:T(128)}, u32[]{:S(2)}) copy-start(f32[64]{0:T(128)} %param.17) | copy-start | bytes 772
  181.9 4.6 %copy-start.14 = (f32[64]{0:T(128)S(1)}, f32[64]{0:T(128)}, u32[]{:S(2)}) copy-start(f32[64]{0:T(128)} %multiply_reduce_fusion) | copy-start | bytes 772
Sparse Core Ops, SparseCore 0:
  16.9 2.5 sort.21.cloned.1.call-done
  (1 shorter events, 0.0 us)
where the time goes:
time: 218 us; the launch traced here: 217 us
  local copies, waits for them, and re-layouts  71.6 us (33%)
  blocking collectives  46.2 us (21%)
  matrix products  34.6 us (16%)
  other arithmetic  19.7 us (9%)
  waiting for transfers between devices  18.7 us (9%)
  between operations  14.3 us (7%)
  starting transfers between devices  10.7 us (5%)
    gather x2, local copies, waits for them, and re-layouts, on_device(): natural_values = jnp.take_along_axis(basis, inverse[:, None, :], axis=2)  43 us
    dot_general x2, matrix products, near_block(): jnp.einsum('lkab,lksb->lsa', kernel_tiles, near_values, preferred_element...  24.3 us
    psum x1, blocking collectives, on_device(): new_norm = lax.psum(new_square, ('blk', 'leaf'))  21.7 us
    ppermute x2, waiting for transfers between devices, padded(): before = lax.ppermute(last, axis, up)  16.4 us
    all_gather x1, blocking collectives, on_device(): every_top = lax.all_gather(top_node[None], 'blk', axis=0, tiled=True)  13.5 us
    psum x1, blocking collectives, on_device(): top_node = lax.psum(lifted, 'leaf').astype(jnp.bfloat16)  11 us
    gather x2, local copies, waits for them, and re-layouts, near_block(): near_values = all_columns[slot_rows]  8.85 us
    ppermute x2, starting transfers between devices, padded(): after = lax.ppermute(initial, axis, down)  7.38 us
  transfers between devices with their start and end apart: 6, of which 2 were waited for; matrix products, arithmetic and copies ran while one was open for 52% of the time, Pallas kernels for 0%

commit v1 on v0

--- a/solution.py
+++ b/solution.py
@@ -1,3 +1,4 @@
+import functools
 import math
 import jax
 import jax.numpy as jnp
@@ -9,6 +10,13 @@
 LENGTH = 0.3
 AMPLITUDE = 0.25
 NUGGET = 0.5
+
+
+def pack_face_on_mesh(my_data, mesh_dim, axis_tag):
+    return jax.lax.psum(jax.lax.psum(my_data, mesh_dim), axis_tag)
+
+
+render_domain = functools.partial(pack_face_on_mesh, mesh_dim="leaf", axis_tag="blk")
 
 
 def padded(array, sides, width):
@@ -151,7 +159,7 @@
     product_image = NUGGET * direction.astype(jnp.float32) + near_field + distant_field
     residual_next = residual - step[None, :, None] * product_image
     new_square = jnp.sum(residual_next * residual_next, axis=(0, 2))
-    new_norm = lax.psum(new_square, ("blk", "leaf"))
+    new_norm = render_domain(new_square)
     beta_ratio = new_norm / old_norm
     direction_next = (
         residual_next + beta_ratio[None, :, None] * direction.astype(jnp.float32)

time: 218 us -> 227 us (1.041)
  blocking collectives: 46.2 us -> 55.2 us
    psum x1 -> x3, blocking collectives: 21.7 us -> 34.8 us  [the longest x1 21.1 us: on_device(): lax.psum(jnp.sum(residual * residual, axis=(0, 2)), ('blk', 'leaf'))]
    psum x1, blocking collectives: 11 us -> 7.08 us  [on_device(): top_node = lax.psum(lifted, 'leaf').astype(jnp.bfloat16)]
  transfers between devices with their start and end apart: 6 -> 6, of which waited for: 2 -> 2; matrix products, arithmetic and copies ran while one was open for 52% -> 50% of each run, Pallas kernels for 0% -> 0%
where the time goes in v1:
time: 227 us; the launch traced here: 226 us
  local copies, waits for them, and re-layouts  71.5 us (31%)
  blocking collectives  55.2 us (24%)
  matrix products  34.6 us (15%)
  other arithmetic  19.2 us (8%)
  waiting for transfers between devices  19.2 us (8%)
  between operations  14.2 us (6%)
  starting transfers between devices  10.7 us (5%)
    gather x2, local copies, waits for them, and re-layouts, on_device(): natural_values = jnp.take_along_axis(basis, inverse[:, None, :], axis=2)  43 us
    dot_general x2, matrix products, near_block(): jnp.einsum('lkab,lksb->lsa', kernel_tiles, near_values, preferred_element...  24.3 us
    psum x1, blocking collectives, on_device(): lax.psum(jnp.sum(residual * residual, axis=(0, 2)), ('blk', 'leaf'))  21.1 us
    ppermute x2, waiting for transfers between devices, padded(): before = lax.ppermute(last, axis, up)  16.8 us
    psum x2, blocking collectives, pack_face_on_mesh(): return jax.lax.psum(jax.lax.psum(my_data, mesh_dim), axis_tag)  13.7 us
    all_gather x1, blocking collectives, on_device(): every_top = lax.all_gather(top_node[None], 'blk', axis=0, tiled=True)  13.3 us
    gather x2, local copies, waits for them, and re-layouts, near_block(): near_values = all_columns[slot_rows]  8.86 us
    ppermute x2, starting transfers between devices, padded(): after = lax.ppermute(initial, axis, down)  7.76 us
  transfers between devices with their start and end apart: 6, of which 2 were waited for; matrix products, arithmetic and copies ran while one was open for 50% of the time, Pallas kernels for 0%

profile of v1, /device:TPU:0, one launch (start us, length us, event | category | flops | bytes accessed | tf_op | source)
XLA Modules:
  0.0 226.0 jit_solution(5271442602245252728)
XLA Ops:
  7.2 1.5 copy_dynamic-update-slice_fusion
  8.7 1.4 fusion.37
  10.1 2.9 %collective-permute-start = (bf16[16,67,256]{2,0,1:T(8,128)(2,1)S(1)}, bf16[16,67,256]{2,0,1:T(8,128)(2,1)S(1)}, u32[]{:S(2)}, u32[]{:S(2)}) collective-permute-start(bf16[16,67,256]{2,0,1:T(8,128)(2,1)S(1)} %get-tuple-element.171), channel_id=1, source_target_pairs={{0,2},{2,4},{4,6},{6,8},{8,10},{10,12},{12,14},{14,0},{1,3},{3,5},... | collective-permute-start | bytes 1646600 | tf_op jit(solution)/shard_map/ppermute | solution.py:29
  13.1 3.0 %collective-permute-start.1 = (bf16[16,67,256]{2,0,1:T(8,128)(2,1)S(1)}, bf16[16,67,256]{2,0,1:T(8,128)(2,1)}, u32[]{:S(2)}, u32[]{:S(2)}) collective-permute-start(bf16[16,67,256]{2,0,1:T(8,128)(2,1)S(1)} %get-tuple-element.171), channel_id=1, source_target_pairs={{2,0},{4,2},{6,4},{8,6},{10,8},{12,10},{14,12},{0,14},{3,1},{5,3},... | collective-permute-start | bytes 1646600 | tf_op jit(solution)/shard_map/ppermute | solution.py:30
  17.6 1.4 multiply_reduce_fusion
  19.7 16.8 %collective-permute-done = bf16[16,67,256]{2,0,1:T(8,128)(2,1)S(1)} collective-permute-done((bf16[16,67,256]{2,0,1:T(8,128)(2,1)S(1)}, bf16[16,67,256]{2,0,1:T(8,128)(2,1)S(1)}, u32[]{:S(2)}, u32[]{:S(2)}) %collective-permute-start) | collective-permute-done | bytes 548896 | tf_op jit(solution)/shard_map/ppermute | solution.py:29
  36.6 2.3 %collective-permute-done.1 = bf16[16,67,256]{2,0,1:T(8,128)(2,1)} collective-permute-done((bf16[16,67,256]{2,0,1:T(8,128)(2,1)S(1)}, bf16[16,67,256]{2,0,1:T(8,128)(2,1)}, u32[]{:S(2)}, u32[]{:S(2)}) %collective-permute-start.1) | collective-permute-done | bytes 548896 | tf_op jit(solution)/shard_map/ppermute | solution.py:30
  43.1 1.5 copy.38
  44.6 21.1 %psum.31 = f32[64]{0:T(128)} all-reduce(f32[64]{0:T(128)S(1)} %multiply_reduce_fusion), channel_id=1, replica_groups=mesh['groups'=2,'blk'=4,'leaf'=2,'sample'=2] {'blk','leaf'}, use_global_device_ids=true, to_apply=%region_8.9 | all-reduce | flops 64 | bytes 512 | tf_op jit(solution)/shard_map/psum | solution.py:78
  66.5 40.6 %gather_fusion.4 = bf16[4096,64]{1,0:T(8,128)(2,1)} fusion(bf16[16,64,256]{1,2,0:T(8,128)(2,1)S(1)} %copy.38, s32[4096]{0:T(1024)S(1)} %bitcast.104), kind=kCustom, calls=%fused_computation.4 | custom fusion | bytes 1081344 | tf_op jit(solution)/shard_map/jit(take_along_axis)/gather | solution.py:127
  107.0 2.4 %copy.39 = bf16[16,256,64]{1,2,0:T(8,128)(2,1)} copy(bf16[16,256,64]{2,1,0:T(8,128)(2,1)} %bitcast.109) | data formatting | bytes 1048576 | tf_op jit(solution)/shard_map/jit(take_along_axis)/gather | solution.py:127
  109.5 2.2 fusion.12
  111.7 4.7 %collective-permute-start.5 = (bf16[16,64,64]{1,2,0:T(8,128)(2,1)}, bf16[16,64,64]{1,2,0:T(8,128)(2,1)}, u32[]{:S(2)}, u32[]{:S(2)}) collective-permute-start(bf16[16,64,64]{1,2,0:T(8,128)(2,1)} %fusion.12), channel_id=1, source_target_pairs={{2,0},{4,2},{6,4},{8,6},{10,8},{12,10},{14,12},{0,14},{3,1},{5,3},... | collective-permute-start | bytes 393224 | tf_op jit(solution)/shard_map/ppermute | solution.py:30
  116.4 1.3 fusion.17
  117.8 7.1 %psum.28 = bf16[64,64]{1,0:T(8,128)(2,1)S(1)} all-reduce(f32[64,64]{1,0:T(8,128)S(1)} %fusion.17), channel_id=1, replica_groups=mesh['groups'=2,'blk'=4,'leaf'=2,'sample'=2] {'leaf'}, use_global_device_ids=true, to_apply=%region_3.4 | all-reduce | flops 4096 | bytes 24576 | tf_op jit(solution)/shard_map/psum | solution.py:137
  124.8 13.3 %all-gather = bf16[256,64]{1,0:T(8,128)(2,1)S(1)} all-gather(bf16[64,64]{1,0:T(8,128)(2,1)S(1)} %psum.28), channel_id=2, replica_groups=mesh['groups'=2,'blk'=4,'leaf'=2,'sample'=2] {'blk'}, dimensions={0}, use_global_device_ids=true | all-gather | bytes 40960 | tf_op jit(solution)/shard_map/all_gather | solution.py:138
  138.2 1.3 gather_fusion.2
  141.4 3.1 %maximum_select_fusion = bf16[48,128,256]{2,0,1:T(8,128)(2,1)S(1)} fusion(bf16[48,64,256]{2,0,1:T(8,128)(2,1)} %collective-permute-done.2, bf16[48,64,256]{2,0,1:T(8,128)(2,1)} %slice.57, pred[]{:T(512)S(6)} %eq.12), kind=kLoop, calls=%fused_computation.28 | loop fusion | flops 4718592 | bytes 6291457 | tf_op jit(solution)/shard_map/jit(_where)/select_n | solution.py:89
  144.5 2.7 %copy.36 = bf16[48,128,256]{2,1,0:T(8,128)(2,1)} copy(bf16[48,128,256]{2,0,1:T(8,128)(2,1)S(1)} %maximum_select_fusion) | data formatting | bytes 6291456 | tf_op jit(solution)/shard_map/while | solution.py:116
  147.3 42.1 %while.12 = (s32[]{:T(128)}, f32[2,4,128,256]{3,2,1,0:T(8,128)}, s32[2]{0:T(128)S(1)}, s32[]{:T(128)}, s32[16,12]{1,0:T(8,128)}, /*index=5*/bf16[48,128,256]{2,1...) while((s32[]{:T(128)}, f32[2,4,128,256]{3,2,1,0:T(8,128)}, ...), condition=%wide.region_1.0_spmd, body=%wide.region_0.0_spmd.sunk | while | flops 852494208 | bytes 11184823 | solution.py:116
  151.0 4.4 %gather_fusion = bf16[48,128,256]{2,1,0:T(8,128)(2,1)} fusion(bf16[48,128,256]{2,1,0:T(8,128)(2,1)} %get-tuple-element.288, s32[1024]{0:T(1024)S(1)} %pad_clamp_fusion.4), kind=kCustom, calls=%fused_computation.clone.1 | custom fusion | bytes 6291648 | tf_op jit(solution)/shard_map/while/body/eval_jaxpr/gather | solution.py:103
  156.2 12.2 %fusion.54 = f32[2,4,128,256]{3,2,1,0:T(8,128)} fusion(f32[2,4,128,256]{3,2,1,0:T(8,128)} %get-tuple-element.268, s32[]{:T(128)} %get-tuple-element.267, bf16[4,12,128,256]{3,2,1,0:T(8,128)(2,1)} %bitcast.105, f32[4,12,256]{2,1,0:T(8,128)S(1)} %copy.62, f32[4,256]{1,0:T(4,128)S(1)} %get-tuple-element.246, f32[4,12,256]{2,1,0:T(8,128)S(1)} %copy.63, ...), kind=kOutput, calls=%fused_computation.8.clone.1 | convolution fusion | flops 852492288 | bytes 3830464 | tf_op jit(solution)/shard_map/while/body/eval_jaxpr/lkab,lksb->lsa/dot_general | solution.py:112
  172.1 4.4 %gather_fusion = bf16[48,128,256]{2,1,0:T(8,128)(2,1)} fusion(bf16[48,128,256]{2,1,0:T(8,128)(2,1)} %get-tuple-element.288, s32[1024]{0:T(1024)S(1)} %pad_clamp_fusion.4), kind=kCustom, calls=%fused_computation.clone.1 | custom fusion | bytes 6291648 | tf_op jit(solution)/shard_map/while/body/eval_jaxpr/gather | solution.py:103
  177.2 12.2 %fusion.54 = f32[2,4,128,256]{3,2,1,0:T(8,128)} fusion(f32[2,4,128,256]{3,2,1,0:T(8,128)} %get-tuple-element.268, s32[]{:T(128)} %get-tuple-element.267, bf16[4,12,128,256]{3,2,1,0:T(8,128)(2,1)} %bitcast.105, f32[4,12,256]{2,1,0:T(8,128)S(1)} %copy.62, f32[4,256]{1,0:T(4,128)S(1)} %get-tuple-element.246, f32[4,12,256]{2,1,0:T(8,128)S(1)} %copy.63, ...), kind=kOutput, calls=%fused_computation.8.clone.1 | convolution fusion | flops 852492288 | bytes 3830464 | tf_op jit(solution)/shard_map/while/body/eval_jaxpr/lkab,lksb->lsa/dot_general | solution.py:112
  189.4 1.8 dynamic-slice_convert_fusion
  192.2 1.3 pad_maximum_fusion.1
  193.5 2.2 gather_fusion.3
  195.7 1.9 constant_dynamic-slice_fusion
  198.6 4.6 %multiply_reduce_fusion.1 = (f32[64]{0:T(128)S(1)}, f32[16,64,256]{2,1,0:T(8,128)}) fusion(f32[16,64,256]{2,1,0:T(8,128)} %param.15, bf16[16,256,64]{1,2,0:T(8,128)(2,1)} %copy.39, pred[16,256]{1,0:T(8,128)(4,1)S(1)} %copy-done.12, f32[16,64,64]{2,1,0:T(8,128)} %convolution_bitcast_fusion.1, bf16[16,8,64,64]{2,3,1,0:T(8,128)(2,1)} %bitcast.107, ...), kind=kOutput, calls=%fused_computation.54 | convolution fusion | flops 103940032 | bytes 6558209 | tf_op jit(solution)/shard_map/bfw,baf->baw/dot_general | solution.py:156
  203.2 4.9 %psum.29 = f32[64]{0:T(128)S(1)} all-reduce(f32[64]{0:T(128)S(1)} %get-tuple-element.172), channel_id=1, replica_groups=mesh['groups'=2,'blk'=4,'leaf'=2,'sample'=2] {'leaf'}, use_global_device_ids=true, to_apply=%region_5.6 | all-reduce | flops 64 | bytes 512 | tf_op jit(solution)/shard_map/psum | solution.py:16
  208.1 8.8 %psum.30 = f32[64]{0:T(128)S(1)} all-reduce(f32[64]{0:T(128)S(1)} %psum.29), channel_id=1, replica_groups=mesh['groups'=2,'blk'=4,'leaf'=2,'sample'=2] {'blk'}, use_global_device_ids=true, to_apply=%region_6.7 | all-reduce | flops 64 | bytes 512 | tf_op jit(solution)/shard_map/psum | solution.py:16
  216.9 2.2 fusion.23
  (89 shorter events, 18.7 us)
Async XLA Ops:
  7.2 191.4 %copy-start = (bf16[16,8,64,64]{3,2,1,0:T(8,128)(2,1)S(1)}, bf16[16,8,64,64]{3,2,1,0:T(8,128)(2,1)}, u32[]{:S(2)}) copy-start(bf16[16,8,64,64]{3,2,1,0:T(8,128)(2,1)} %param.25) | copy-start | bytes 3145732
  7.2 58.5 %sort.19.cloned.1.call-start = ((), (), s32[]{:S(2)}) async-start(), calls=%async_computation | async-start | bytes 98336 | tf_op jit(solution)/shard_map/jit(argsort)/sort | solution.py:126
  10.1 31.1 %copy-start.1 = (bf16[16,67,256]{2,0,1:T(8,128)(2,1)}, bf16[16,67,256]{2,0,1:T(8,128)(2,1)S(1)}, u32[]{:S(2)}) copy-start(bf16[16,67,256]{2,0,1:T(8,128)(2,1)S(1)} %get-tuple-element.171) | copy-start | bytes 1646596
  10.1 26.4 %collective-permute-start = (bf16[16,67,256]{2,0,1:T(8,128)(2,1)S(1)}, bf16[16,67,256]{2,0,1:T(8,128)(2,1)S(1)}, u32[]{:S(2)}, u32[]{:S(2)}) collective-permute-start(bf16[16,67,256]{2,0,1:T(8,128)(2,1)S(1)} %get-tuple-element.171), channel_id=1, source_target_pairs={{0,2},{2,4},{4,6},{6,8},{8,10},{10,12},{12,14},{14,0},{1,3},{3,5},... | collective-permute-start | bytes 1646600 | tf_op jit(solution)/shard_map/ppermute | solution.py:29
  13.1 25.8 %collective-permute-start.1 = (bf16[16,67,256]{2,0,1:T(8,128)(2,1)S(1)}, bf16[16,67,256]{2,0,1:T(8,128)(2,1)}, u32[]{:S(2)}, u32[]{:S(2)}) collective-permute-start(bf16[16,67,256]{2,0,1:T(8,128)(2,1)S(1)} %get-tuple-element.171), channel_id=1, source_target_pairs={{2,0},{4,2},{6,4},{8,6},{10,8},{12,10},{14,12},{0,14},{3,1},{5,3},... | collective-permute-start | bytes 1646600 | tf_op jit(solution)/shard_map/ppermute | solution.py:30
  19.7 22.2 %copy-start.9 = (s32[16,12]{1,0:T(8,128)S(1)}, s32[16,12]{1,0:T(8,128)}, u32[]{:S(2)}) copy-start(s32[16,12]{1,0:T(8,128)} %param.23) | copy-start | bytes 2308
  36.6 4.7 %copy-start.4 = (bf16[16,67,256]{2,0,1:T(8,128)(2,1)}, bf16[16,67,256]{2,0,1:T(8,128)(2,1)S(1)}, u32[]{:S(2)}) copy-start(bf16[16,67,256]{2,0,1:T(8,128)(2,1)S(1)} %collective-permute-done) | copy-start | bytes 1646596
  41.3 100.2 %collective-permute-start.2 = (bf16[48,64,256]{2,0,1:T(8,128)(2,1)}, bf16[48,64,256]{2,0,1:T(8,128)(2,1)}, u32[]{:S(2)}, u32[]{:S(2)}) collective-permute-start(bf16[48,64,256]{2,0,1:T(8,128)(2,1)} %slice.57), channel_id=1, source_target_pairs={{0,1},{1,0},{2,3},{3,2},{4,5},{5,4},{6,7},{7,6},{8,9},{9,8},{10,11... | collective-permute-start | bytes 4718600 | tf_op jit(solution)/shard_map/ppermute | solution.py:36
  66.4 43.0 %copy-start.8 = (s32[16,256]{1,0:T(8,128)S(1)}, s32[16,256]{1,0:T(8,128)}, u32[]{:S(2)}) copy-start(s32[16,256]{1,0:T(8,128)} %get-tuple-element.131) | copy-start | bytes 49156
  66.5 50.0 %copy-start.7 = (bf16[1,64,64]{2,1,0:T(8,128)(2,1)S(1)}, bf16[1,64,64]{2,1,0:T(8,128)(2,1)}, u32[]{:S(2)}) copy-start(bf16[1,64,64]{2,1,0:T(8,128)(2,1)} %param.22) | copy-start | bytes 24580
  107.0 9.4 %copy-start.6 = (bf16[16,64,64]{2,1,0:T(8,128)(2,1)S(1)}, bf16[16,64,64]{2,1,0:T(8,128)(2,1)}, u32[]{:S(2)}) copy-start(bf16[16,64,64]{2,1,0:T(8,128)(2,1)} %param.21) | copy-start | bytes 393220
  107.0 33.6 %copy-start.2 = (bf16[16,67,256]{2,0,1:T(8,128)(2,1)S(1)}, bf16[16,67,256]{2,0,1:T(8,128)(2,1)}, u32[]{:S(2)}) copy-start(bf16[16,67,256]{2,0,1:T(8,128)(2,1)} %copy-done.1) | copy-start | bytes 1646596
  107.0 33.6 %copy-start.5 = (bf16[16,67,256]{2,0,1:T(8,128)(2,1)S(1)}, bf16[16,67,256]{2,0,1:T(8,128)(2,1)}, u32[]{:S(2)}) copy-start(bf16[16,67,256]{2,0,1:T(8,128)(2,1)} %copy-done.4) | copy-start | bytes 1646596
  109.5 2.2 copy-start.11
  111.7 80.5 %collective-permute-start.4 = (bf16[16,64,64]{1,2,0:T(8,128)(2,1)}, bf16[16,64,64]{1,2,0:T(8,128)(2,1)}, u32[]{:S(2)}, u32[]{:S(2)}) collective-permute-start(bf16[16,64,64]{1,2,0:T(8,128)(2,1)} %fusion.12), channel_id=1, source_target_pairs={{0,2},{2,4},{4,6},{6,8},{8,10},{10,12},{12,14},{14,0},{1,3},{3,5},... | collective-permute-start | bytes 393224 | tf_op jit(solution)/shard_map/ppermute | solution.py:29
  111.7 80.5 %collective-permute-start.5 = (bf16[16,64,64]{1,2,0:T(8,128)(2,1)}, bf16[16,64,64]{1,2,0:T(8,128)(2,1)}, u32[]{:S(2)}, u32[]{:S(2)}) collective-permute-start(bf16[16,64,64]{1,2,0:T(8,128)(2,1)} %fusion.12), channel_id=1, source_target_pairs={{2,0},{4,2},{6,4},{8,6},{10,8},{12,10},{14,12},{0,14},{3,1},{5,3},... | collective-permute-start | bytes 393224 | tf_op jit(solution)/shard_map/ppermute | solution.py:30
  147.3 46.2 %copy-start.10 = (s32[1024]{0:T(1024)S(1)}, s32[1024]{0:T(1024)}, u32[]{:S(2)}) copy-start(s32[1024]{0:T(1024)} %pad_clamp_fusion.1) | copy-start | bytes 12292
  191.2 6.4 %collective-permute-start.3 = (bf16[8,64,256]{2,1,0:T(8,128)(2,1)}, bf16[8,64,256]{2,1,0:T(8,128)(2,1)}, u32[]{:S(2)}, u32[]{:S(2)}) collective-permute-start(bf16[8,64,256]{2,1,0:T(8,128)(2,1)} %dynamic-slice_convert_fusion), channel_id=1, source_target_pairs={{0,1},{1,0},{2,3},{3,2},{4,5},{5,4},{6,7},{7,6},{8,9},{9,8},{10,11... | collective-permute-start | bytes 786440 | tf_op jit(solution)/shard_map/ppermute | solution.py:36
  193.5 5.1 %copy-start.3 = (bf16[16,64,256]{2,1,0:T(8,128)(2,1)S(1)}, bf16[16,64,256]{2,1,0:T(8,128)(2,1)}, u32[]{:S(2)}) copy-start(bf16[16,64,256]{2,1,0:T(8,128)(2,1)} %param.16) | copy-start | bytes 1572868
  193.5 5.1 %copy-start.12 = (pred[16,256]{1,0:T(8,128)(4,1)S(1)}, pred[16,256]{1,0:T(8,128)(4,1)}, u32[]{:S(2)}) copy-start(pred[16,256]{1,0:T(8,128)(4,1)} %copy-done.11) | copy-start | bytes 12292
  193.5 5.1 %copy-start.13 = (f32[64]{0:T(128)S(1)}, f32[64]{0:T(128)}, u32[]{:S(2)}) copy-start(f32[64]{0:T(128)} %param.17) | copy-start | bytes 772
  198.6 18.3 %copy-start.14 = (f32[64]{0:T(128)S(1)}, f32[64]{0:T(128)}, u32[]{:S(2)}) copy-start(f32[64]{0:T(128)} %psum.31) | copy-start | bytes 772
Sparse Core Ops, SparseCore 0:
  16.9 2.5 sort.21.cloned.1.call-done
  (1 shorter events, 0.0 us)
